TPU v7x, 256 devices: a whole 4x4x8 slice. The times are simulated.
256 devices in a mesh: stream: 4 (over x), seq: 64 (over z, y, core).
Axes of the slice: x: 4, y: 4, z: 8, core: 2. Of those that a mesh axis runs over, the one named last changes fastest.
Arguments:
- inputs: bfloat16 [4, 8192, 2048], P('stream', 'seq'), may hold values from -16 to 16
- cotangent: bfloat16 [4, 8192, 2048], P('stream', 'seq'), may hold values from -6 to 6
- lengths: int32 [4, 4], P('stream'), may hold values from 1 to 6144, 8192 in all within a row
- angles: float32 [2, 2048], replicated, may hold values from -3.140625 to 3.140625
- mix: float32 [14, 2048], replicated, may hold values from -1.5 to 1.5
- weight: bfloat16 [2048, 2048], replicated, may hold values from -0.125 to 0.125
Outputs:
- output: bfloat16 [4, 8192, 2048], P('stream', 'seq')
- input_grad: bfloat16 [4, 8192, 2048], P('stream', 'seq')
- weight_grad: float32 [2048, 2048], P('seq')
- angle_grad: float32 [2, 2048], replicated
- mix_grad: float32 [14, 2048], replicated
Inputs may be any that keep to these rules, and one draw needn't show every extreme that they name: Each row holds the lengths of the 4 documents of one stream in time order; they sum to 8192, and the longest is exactly 6144.
All inputs are finite; a program needn't handle non-finite values.
Results may differ from a plain program's by a relative error of at most 0.012.
Values may be sent and summed in bfloat16 or wider, within the bound.
No kernel may reach another device: no remote copies, remote signals or barrier semaphores. Data moves between devices by JAX's collectives and lax.ppermute only.
A program may use at most 128 MiB of HBM per device.

v0:
```python
import jax
import jax.numpy as jnp
from jax import lax
from jax.sharding import PartitionSpec as P


def from_behind(block, axis, distance):
    devices = range(lax.axis_size(axis))
    route = [(i - distance, i) for i in devices if i - distance in devices]
    return lax.ppermute(block, axis, route)


def segment_start(lengths_row, times):
    ends = jnp.cumsum(lengths_row, dtype=jnp.int32)
    hits = jnp.where(ends[None, :] <= times[:, None], lengths_row[None, :], 0)
    return jnp.sum(hits, axis=1, dtype=jnp.int32)


def tap_mask(times, start, dist):
    return (times - dist >= start).astype(jnp.float32)


def body(inputs, cotangent, lengths, angles, mix, weight):
    local_in = inputs[0]
    local_cot = cotangent[0]
    rows, width = local_in.shape
    seq_count = lax.axis_size("seq")
    stream_count = lax.axis_size("stream")
    far_count = seq_count.bit_length() - 1
    near_count = rows.bit_length() - 1
    levels = near_count + far_count
    total = rows * seq_count
    factor = float(stream_count * total) ** (-0.5)
    member = lax.axis_index("seq")
    cos_a = jnp.cos(angles[0])
    sin_a = jnp.sin(angles[0])
    cos_d = jnp.cos(angles[1])
    sin_d = jnp.sin(angles[1])
    times = member * rows + jnp.arange(rows, dtype=jnp.int32)
    start = segment_start(lengths[0], times)
    masks = [tap_mask(times, start, 2**level)[:, None] for level in range(levels)]
    current = local_in
    stored = [current]
    taps = []
    mixed = jnp.zeros((rows, width), jnp.float32)
    for level in range(near_count):
        dist = 2**level
        before = from_behind(current[rows - dist :], "seq", 1)
        shifted = (
            jnp.concatenate([before, current[: rows - dist]], axis=0).astype(jnp.float32)
            * masks[level]
        )
        plain = current.astype(jnp.float32)
        mixed = mixed + mix[level] * (cos_d * plain + sin_d * shifted)
        current = lax.optimization_barrier((cos_a * plain + sin_a * shifted).astype(jnp.bfloat16))
        taps.append(shifted.astype(jnp.bfloat16))
        stored.append(current)
    for level in range(near_count, levels):
        dist = 2**level
        arrived = from_behind(current, "seq", dist // rows)
        shifted = arrived.astype(jnp.float32) * masks[level]
        plain = current.astype(jnp.float32)
        mixed = mixed + mix[level] * (cos_d * plain + sin_d * shifted)
        current = lax.optimization_barrier((cos_a * plain + sin_a * shifted).astype(jnp.bfloat16))
        taps.append(shifted.astype(jnp.bfloat16))
        stored.append(current)
    mixed = mixed + mix[levels] * current.astype(jnp.float32)
    act = jax.nn.gelu(mixed).astype(jnp.bfloat16)
    output = jnp.dot(act, weight, preferred_element_type=jnp.float32).astype(jnp.bfloat16)
    act_grad = lax.optimization_barrier(
        lax.dot_general(
            local_cot, weight, (((1,), (1,)), ((), ())), preferred_element_type=jnp.float32
        ).astype(jnp.bfloat16)
    )
    unused, pull = jax.vjp(jax.nn.gelu, mixed)
    mixed_grad = lax.optimization_barrier(
        pull(act_grad.astype(jnp.float32))[0].astype(jnp.bfloat16)
    )
    grad_full = mixed_grad.astype(jnp.float32)
    upper = mix[levels] * grad_full
    mix_rows = [None] * (levels + 1)
    mix_rows[levels] = jnp.sum(grad_full * stored[levels].astype(jnp.float32), axis=0)
    theta = jnp.zeros((width,), jnp.float32)
    phi = jnp.zeros((width,), jnp.float32)
    carried = stored[0]
    for level in reversed(range(levels)):
        dist = 2**level
        plain = stored[level].astype(jnp.float32)
        shifted = taps[level].astype(jnp.float32)
        along = mix[level] * grad_full
        mix_rows[level] = jnp.sum(grad_full * (cos_d * plain + sin_d * shifted), axis=0)
        theta = theta + jnp.sum(upper * (cos_a * shifted - sin_a * plain), axis=0)
        phi = phi + jnp.sum(along * (cos_d * shifted - sin_d * plain), axis=0)
        sent = lax.optimization_barrier(
            (masks[level] * (sin_a * upper + sin_d * along)).astype(jnp.bfloat16)
        )
        if dist < rows:
            after = from_behind(sent[:dist], "seq", -1)
            back = jnp.concatenate([sent[dist:], after], axis=0)
        else:
            back = from_behind(sent, "seq", -(dist // rows))
        carried = lax.optimization_barrier(
            (cos_a * upper + cos_d * along + back.astype(jnp.float32)).astype(jnp.bfloat16)
        )
        upper = carried.astype(jnp.float32)
    angle_all, mix_all = lax.psum((jnp.stack([theta, phi]), jnp.stack(mix_rows)), ("stream", "seq"))
    weight_rows = lax.psum_scatter(
        lax.dot_general(
            act, local_cot, (((0,), (0,)), ((), ())), preferred_element_type=jnp.float32
        ),
        "seq",
        scatter_dimension=0,
        tiled=True,
    )
    weight_rows = lax.psum(weight_rows, "stream")
    return (output[None], carried[None], weight_rows * factor, angle_all * factor, mix_all * factor)


def solution(mesh):
    in_specs = (
        P("stream", "seq", None),
        P("stream", "seq", None),
        P("stream", None),
        P(),
        P(),
        P(),
    )
    out_specs = (P("stream", "seq", None), P("stream", "seq", None), P("seq", None), P(), P())
    return jax.shard_map(body, mesh=mesh, in_specs=in_specs, out_specs=out_specs, check_vma=False)
```

profile of v0, /device:TPU:8, one launch (start us, length us, event | category | flops | bytes accessed | tf_op | source)
XLA Modules:
  0.0 812.0 jit_solution(9908100230172136991)
XLA Ops:
  17.4 3.6 collective-permute-start.1
  25.5 3.1 collective-permute-done.2
  31.6 3.3 collective-permute-done.3
  35.9 2.1 collective-permute-start.4
  38.0 3.6 collective-permute-done.4
  44.5 4.3 collective-permute-done.5
  51.7 5.8 collective-permute-done.6
  58.5 2.1 collective-permute-start.7
  60.6 8.6 %collective-permute-done.7 = bf16[128,2048]{1,0:T(8,128)(2,1)S(1)} collective-permute-done((bf16[128,2048]{1,0:T(8,128)(2,1)S(1)}, bf16[128,2048]{1,0:T(8,128)(2,1)S(1)}, u32[]{:S(2)}, u32[]{:S(2)}) %collective-permute-start.7) | collective-permute-done | bytes 524320 | tf_op jit(solution)/shard_map/ppermute | solution.py:10
  70.1 3.5 collective-permute-start.8
  73.6 11.4 %collective-permute-done.8 = bf16[128,2048]{1,0:T(8,128)(2,1)S(1)} collective-permute-done((bf16[128,2048]{1,0:T(8,128)(2,1)S(1)}, bf16[128,2048]{1,0:T(8,128)(2,1)S(1)}, u32[]{:S(2)}, u32[]{:S(2)}) %collective-permute-start.8) | collective-permute-done | bytes 524320 | tf_op jit(solution)/shard_map/ppermute | solution.py:10
  86.0 15.0 %collective-permute-start.9 = (bf16[128,2048]{1,0:T(8,128)(2,1)S(1)}, bf16[128,2048]{1,0:T(8,128)(2,1)S(1)}, u32[]{:S(2)}, u32[]{:S(2)}) collective-permute-start(bf16[128,2048]{1,0:T(8,128)(2,1)S(1)} %fusion.250), channel_id=1, source_target_pairs={{0,4},{1,5},{2,6},{3,7},{4,8},{5,9},{6,10},{7,11},{8,12},{9,13},{1... | collective-permute-start | bytes 1572872 | tf_op jit(solution)/shard_map/ppermute | solution.py:10
  101.0 7.5 collective-permute-done.9
  109.4 4.3 collective-permute-start.10
  113.8 6.6 collective-permute-done.10
  121.4 14.6 %collective-permute-start.11 = (bf16[128,2048]{1,0:T(8,128)(2,1)S(1)}, bf16[128,2048]{1,0:T(8,128)(2,1)S(1)}, u32[]{:S(2)}, u32[]{:S(2)}) collective-permute-start(bf16[128,2048]{1,0:T(8,128)(2,1)S(1)} %fusion.254), channel_id=1, source_target_pairs={{0,16},{1,17},{2,18},{3,19},{4,20},{5,21},{6,22},{7,23},{8,24},{9,... | collective-permute-start | bytes 1572872 | tf_op jit(solution)/shard_map/ppermute | solution.py:10
  136.0 8.1 collective-permute-done.11
  145.0 31.3 %collective-permute-start.12 = (bf16[128,2048]{1,0:T(8,128)(2,1)S(1)}, bf16[128,2048]{1,0:T(8,128)(2,1)S(1)}, u32[]{:S(2)}, u32[]{:S(2)}) collective-permute-start(bf16[128,2048]{1,0:T(8,128)(2,1)S(1)} %fusion.256), channel_id=1, source_target_pairs={{0,32},{1,33},{2,34},{3,35},{4,36},{5,37},{6,38},{7,39},{8,40},{9,... | collective-permute-start | bytes 1572872 | tf_op jit(solution)/shard_map/ppermute | solution.py:10
  176.4 2.9 convolution_convert_fusion
  179.5 7.8 collective-permute-done.12
  188.4 7.4 fusion.97
  197.1 8.1 %fusion.288 = f32[2048,2048]{1,0:T(8,128)} fusion(bf16[1,128,2048]{2,1,0:T(8,128)(2,1)S(1)} %copy-done, f32[128,2048]{1,0:T(8,128)S(1)} %get-tuple-element.55), kind=kOutput, calls=%fused_computation.471 | convolution fusion | flops 1076101120 | bytes 18350080 | tf_op jit(solution)/shard_map/dot_general | solution.py:108
  208.0 19.3 %collective-permute-done.13 = bf16[128,2048]{1,0:T(8,128)(2,1)S(1)} collective-permute-done((bf16[128,2048]{1,0:T(8,128)(2,1)S(1)}, bf16[128,2048]{1,0:T(8,128)(2,1)S(1)}, u32[]{:S(2)}, u32[]{:S(2)}) %collective-permute-start.13) | collective-permute-done | bytes 524320 | tf_op jit(solution)/shard_map/ppermute | solution.py:10
  230.6 26.2 %collective-permute-done.14 = bf16[128,2048]{1,0:T(8,128)(2,1)S(1)} collective-permute-done((bf16[128,2048]{1,0:T(8,128)(2,1)S(1)}, bf16[128,2048]{1,0:T(8,128)(2,1)S(1)}, u32[]{:S(2)}, u32[]{:S(2)}) %collective-permute-start.14) | collective-permute-done | bytes 524320 | tf_op jit(solution)/shard_map/ppermute | solution.py:10
  260.5 13.7 %collective-permute-done.15 = bf16[128,2048]{1,0:T(8,128)(2,1)S(1)} collective-permute-done((bf16[128,2048]{1,0:T(8,128)(2,1)S(1)}, bf16[128,2048]{1,0:T(8,128)(2,1)S(1)}, u32[]{:S(2)}, u32[]{:S(2)}) %collective-permute-start.15) | collective-permute-done | bytes 524320 | tf_op jit(solution)/shard_map/ppermute | solution.py:10
  275.4 3.1 fusion.270
  279.7 19.8 %collective-permute-done.16 = bf16[128,2048]{1,0:T(8,128)(2,1)S(1)} collective-permute-done((bf16[128,2048]{1,0:T(8,128)(2,1)S(1)}, bf16[128,2048]{1,0:T(8,128)(2,1)S(1)}, u32[]{:S(2)}, u32[]{:S(2)}) %collective-permute-start.16) | collective-permute-done | bytes 524320 | tf_op jit(solution)/shard_map/ppermute | solution.py:10
  299.9 3.1 fusion.269
  303.0 10.8 %collective-permute-start.17 = (bf16[128,2048]{1,0:T(8,128)(2,1)S(1)}, bf16[128,2048]{1,0:T(8,128)(2,1)S(1)}, u32[]{:S(2)}, u32[]{:S(2)}) collective-permute-start(bf16[128,2048]{1,0:T(8,128)(2,1)S(1)} %get-tuple-element.57), channel_id=1, source_target_pairs={{2,0},{3,1},{4,2},{5,3},{6,4},{7,5},{8,6},{9,7},{10,8},{11,9},{12,... | collective-permute-start | bytes 1572872 | tf_op jit(solution)/shard_map/ppermute | solution.py:10
  313.9 22.7 %collective-permute-done.17 = bf16[128,2048]{1,0:T(8,128)(2,1)S(1)} collective-permute-done((bf16[128,2048]{1,0:T(8,128)(2,1)S(1)}, bf16[128,2048]{1,0:T(8,128)(2,1)S(1)}, u32[]{:S(2)}, u32[]{:S(2)}) %collective-permute-start.17) | collective-permute-done | bytes 524320 | tf_op jit(solution)/shard_map/ppermute | solution.py:10
  337.0 3.0 fusion.268
  341.9 6.7 collective-permute-done.18
  348.9 2.2 fusion.267
  351.2 4.2 collective-permute-start.19
  355.4 3.9 collective-permute-done.19
  359.6 2.2 fusion.266
  361.8 4.2 collective-permute-start.20
  366.1 5.5 collective-permute-done.20
  373.5 3.4 collective-permute-start.21
  376.9 5.1 collective-permute-done.21
  386.0 3.6 collective-permute-done.22
  393.8 3.1 collective-permute-done.23
  399.2 2.1 collective-permute-start.24
  401.3 2.3 fusion
  406.6 2.2 collective-permute-start.25
  408.9 101.6 %psum.22 = f32[2,2048]{1,0:T(2,128)S(1)} all-reduce(f32[2,2048]{1,0:T(2,128)S(1)} %pad_maximum_fusion.7), channel_id=1, replica_groups=mesh['stream'=4,'seq'=64] {'stream','seq'}, use_global_device_ids=true, to_apply=%region_30.31 | all-reduce | flops 4096 | bytes 32768 | tf_op jit(solution)/shard_map/psum | solution.py:106
  514.0 243.3 %all-reduce.5.cloned.1.call-done = f32[14,2048]{1,0:T(8,128)} async-done(((f32[14,2048]{1,0:T(8,128)}), f32[14,2048]{1,0:T(8,128)}) %all-reduce.5.cloned.1.call-update) | async-done | bytes 114704 | tf_op jit(solution)/shard_map/psum | solution.py:106
  758.8 43.9 %all-reduce.3.cloned.1.call-done = f32[32,2048]{1,0:T(8,128)} async-done(((f32[32,2048]{1,0:T(8,128)}), f32[32,2048]{1,0:T(8,128)}) %all-reduce.3.cloned.1.call-update) | async-done | bytes 262160 | tf_op jit(solution)/shard_map/psum | solution.py:115
  (302 shorter events, 68.1 us)
Async XLA Ops:
  8.0 168.4 %copy-start = (bf16[1,128,2048]{2,1,0:T(8,128)(2,1)S(1)}, bf16[1,128,2048]{2,1,0:T(8,128)(2,1)}, u32[]{:S(2)}) copy-start(bf16[1,128,2048]{2,1,0:T(8,128)(2,1)} %param.7) | copy-start | bytes 1572868
  8.0 505.9 %reduce-scatter.2.cloned.1.call-start = ((), (), s32[]{:S(2)}) async-start(), calls=%async_computation.1 | async-start | bytes 17039360 | tf_op jit(solution)/shard_map/reduce_scatter | solution.py:107
  8.9 7.1 collective-permute-start
  17.4 5.1 collective-permute-start.1
  23.6 5.1 collective-permute-start.2
  28.6 159.6 %copy-start.65 = (bf16[4,2048]{1,0:T(4,128)(2,1)}, bf16[4,2048]{1,0:T(4,128)(2,1)S(1)}, u32[]{:S(2)}) copy-start(bf16[4,2048]{1,0:T(4,128)(2,1)S(1)} %collective-permute-done.2) | copy-start | bytes 49156
  29.7 5.2 collective-permute-start.3
  31.6 156.6 %copy-start.22 = (bf16[120,2048]{1,0:T(8,128)(2,1)}, bf16[120,2048]{1,0:T(8,128)(2,1)S(1)}, u32[]{:S(2)}) copy-start(bf16[120,2048]{1,0:T(8,128)(2,1)S(1)} %slice.205) | copy-start | bytes 1474564
  34.9 153.4 %copy-start.55 = (bf16[8,2048]{1,0:T(8,128)(2,1)}, bf16[8,2048]{1,0:T(8,128)(2,1)S(1)}, u32[]{:S(2)}) copy-start(bf16[8,2048]{1,0:T(8,128)(2,1)S(1)} %collective-permute-done.3) | copy-start | bytes 98308
  34.9 141.5 %slice-start = ((s8[8388608]{0:T(1024)(128)(4,1)}), s8[4194304]{0:T(1024)(128)(4,1)S(1)}, s32[]{:S(2)}) async-start(s8[8388608]{0:T(1024)(128)(4,1)} %bitcast.103), calls=%async_computation.4 | async-start | bytes 8388608
  35.9 5.7 collective-permute-start.4
  38.0 150.2 %copy-start.24 = (bf16[112,2048]{1,0:T(8,128)(2,1)}, bf16[112,2048]{1,0:T(8,128)(2,1)S(1)}, u32[]{:S(2)}) copy-start(bf16[112,2048]{1,0:T(8,128)(2,1)S(1)} %slice.207) | copy-start | bytes 1376260
  41.7 146.6 %copy-start.53 = (bf16[16,2048]{1,0:T(8,128)(2,1)}, bf16[16,2048]{1,0:T(8,128)(2,1)S(1)}, u32[]{:S(2)}) copy-start(bf16[16,2048]{1,0:T(8,128)(2,1)S(1)} %collective-permute-done.4) | copy-start | bytes 196612
  42.5 145.8 %copy-start.1 = (bf16[128,2048]{1,0:T(8,128)(2,1)}, bf16[128,2048]{1,0:T(8,128)(2,1)S(1)}, u32[]{:S(2)}) copy-start(bf16[128,2048]{1,0:T(8,128)(2,1)S(1)} %fusion.242) | copy-start | bytes 1572868
  42.6 6.3 collective-permute-start.5
  48.8 139.5 %copy-start.51 = (bf16[32,2048]{1,0:T(8,128)(2,1)}, bf16[32,2048]{1,0:T(8,128)(2,1)S(1)}, u32[]{:S(2)}) copy-start(bf16[32,2048]{1,0:T(8,128)(2,1)S(1)} %collective-permute-done.5) | copy-start | bytes 393220
  49.7 138.6 %copy-start.3 = (bf16[128,2048]{1,0:T(8,128)(2,1)}, bf16[128,2048]{1,0:T(8,128)(2,1)S(1)}, u32[]{:S(2)}) copy-start(bf16[128,2048]{1,0:T(8,128)(2,1)S(1)} %fusion.244) | copy-start | bytes 1572868
  49.8 138.6 %copy-start.43 = (bf16[64,2048]{1,0:T(8,128)(2,1)}, bf16[64,2048]{1,0:T(8,128)(2,1)S(1)}, u32[]{:S(2)}) copy-start(bf16[64,2048]{1,0:T(8,128)(2,1)S(1)} %get-tuple-element.69) | copy-start | bytes 786436
  49.8 7.7 collective-permute-start.6
  57.5 130.9 %copy-start.47 = (bf16[64,2048]{1,0:T(8,128)(2,1)}, bf16[64,2048]{1,0:T(8,128)(2,1)S(1)}, u32[]{:S(2)}) copy-start(bf16[64,2048]{1,0:T(8,128)(2,1)S(1)} %collective-permute-done.6) | copy-start | bytes 786436
  57.5 118.9 %slice-start.1 = ((s8[8388608]{0:T(1024)(128)(4,1)}), s8[4194304]{0:T(1024)(128)(4,1)S(1)}, s32[]{:S(2)}) async-start(s8[8388608]{0:T(1024)(128)(4,1)} %bitcast.103), calls=%async_computation.5 | async-start | bytes 8388608
  58.5 129.9 %copy-start.18 = (bf16[128,2048]{1,0:T(8,128)(2,1)}, bf16[128,2048]{1,0:T(8,128)(2,1)S(1)}, u32[]{:S(2)}) copy-start(bf16[128,2048]{1,0:T(8,128)(2,1)S(1)} %fusion.246) | copy-start | bytes 1572868
  58.5 10.6 %collective-permute-start.7 = (bf16[128,2048]{1,0:T(8,128)(2,1)S(1)}, bf16[128,2048]{1,0:T(8,128)(2,1)S(1)}, u32[]{:S(2)}, u32[]{:S(2)}) collective-permute-start(bf16[128,2048]{1,0:T(8,128)(2,1)S(1)} %fusion.246), channel_id=1, source_target_pairs={{0,1},{1,2},{2,3},{3,4},{4,5},{5,6},{6,7},{7,8},{8,9},{9,10},{10,1... | collective-permute-start | bytes 1572872 | tf_op jit(solution)/shard_map/ppermute | solution.py:10
  69.1 119.2 %copy-start.39 = (bf16[128,2048]{1,0:T(8,128)(2,1)}, bf16[128,2048]{1,0:T(8,128)(2,1)S(1)}, u32[]{:S(2)}) copy-start(bf16[128,2048]{1,0:T(8,128)(2,1)S(1)} %collective-permute-done.7) | copy-start | bytes 1572868
  70.1 118.3 %copy-start.7 = (bf16[128,2048]{1,0:T(8,128)(2,1)}, bf16[128,2048]{1,0:T(8,128)(2,1)S(1)}, u32[]{:S(2)}) copy-start(bf16[128,2048]{1,0:T(8,128)(2,1)S(1)} %fusion.248) | copy-start | bytes 1572868
  70.1 14.9 %collective-permute-start.8 = (bf16[128,2048]{1,0:T(8,128)(2,1)S(1)}, bf16[128,2048]{1,0:T(8,128)(2,1)S(1)}, u32[]{:S(2)}, u32[]{:S(2)}) collective-permute-start(bf16[128,2048]{1,0:T(8,128)(2,1)S(1)} %fusion.248), channel_id=1, source_target_pairs={{0,2},{1,3},{2,4},{3,5},{4,6},{5,7},{6,8},{7,9},{8,10},{9,11},{10,... | collective-permute-start | bytes 1572872 | tf_op jit(solution)/shard_map/ppermute | solution.py:10
  86.0 22.5 %collective-permute-start.9 = (bf16[128,2048]{1,0:T(8,128)(2,1)S(1)}, bf16[128,2048]{1,0:T(8,128)(2,1)S(1)}, u32[]{:S(2)}, u32[]{:S(2)}) collective-permute-start(bf16[128,2048]{1,0:T(8,128)(2,1)S(1)} %fusion.250), channel_id=1, source_target_pairs={{0,4},{1,5},{2,6},{3,7},{4,8},{5,9},{6,10},{7,11},{8,12},{9,13},{1... | collective-permute-start | bytes 1572872 | tf_op jit(solution)/shard_map/ppermute | solution.py:10
  109.4 11.0 %collective-permute-start.10 = (bf16[128,2048]{1,0:T(8,128)(2,1)S(1)}, bf16[128,2048]{1,0:T(8,128)(2,1)S(1)}, u32[]{:S(2)}, u32[]{:S(2)}) collective-permute-start(bf16[128,2048]{1,0:T(8,128)(2,1)S(1)} %fusion.252), channel_id=1, source_target_pairs={{0,8},{1,9},{2,10},{3,11},{4,12},{5,13},{6,14},{7,15},{8,16},{9,17... | collective-permute-start | bytes 1572872 | tf_op jit(solution)/shard_map/ppermute | solution.py:10
  121.4 22.7 %collective-permute-start.11 = (bf16[128,2048]{1,0:T(8,128)(2,1)S(1)}, bf16[128,2048]{1,0:T(8,128)(2,1)S(1)}, u32[]{:S(2)}, u32[]{:S(2)}) collective-permute-start(bf16[128,2048]{1,0:T(8,128)(2,1)S(1)} %fusion.254), channel_id=1, source_target_pairs={{0,16},{1,17},{2,18},{3,19},{4,20},{5,21},{6,22},{7,23},{8,24},{9,... | collective-permute-start | bytes 1572872 | tf_op jit(solution)/shard_map/ppermute | solution.py:10
  145.0 42.4 %collective-permute-start.12 = (bf16[128,2048]{1,0:T(8,128)(2,1)S(1)}, bf16[128,2048]{1,0:T(8,128)(2,1)S(1)}, u32[]{:S(2)}, u32[]{:S(2)}) collective-permute-start(bf16[128,2048]{1,0:T(8,128)(2,1)S(1)} %fusion.256), channel_id=1, source_target_pairs={{0,32},{1,33},{2,34},{3,35},{4,36},{5,37},{6,38},{7,39},{8,40},{9,... | collective-permute-start | bytes 1572872 | tf_op jit(solution)/shard_map/ppermute | solution.py:10
  205.2 552.0 %all-reduce.5.cloned.1.call-start = ((), (), s32[]{:S(2)}) async-start(), calls=%async_computation.3 | async-start | bytes 262144 | tf_op jit(solution)/shard_map/psum | solution.py:106
  206.6 20.8 %collective-permute-start.13 = (bf16[128,2048]{1,0:T(8,128)(2,1)S(1)}, bf16[128,2048]{1,0:T(8,128)(2,1)S(1)}, u32[]{:S(2)}, u32[]{:S(2)}) collective-permute-start(bf16[128,2048]{1,0:T(8,128)(2,1)S(1)} %fusion.189), channel_id=1, source_target_pairs={{32,0},{33,1},{34,2},{35,3},{36,4},{37,5},{38,6},{39,7},{40,8},{41... | collective-permute-start | bytes 1572872 | tf_op jit(solution)/shard_map/ppermute | solution.py:10
  229.3 27.5 %collective-permute-start.14 = (bf16[128,2048]{1,0:T(8,128)(2,1)S(1)}, bf16[128,2048]{1,0:T(8,128)(2,1)S(1)}, u32[]{:S(2)}, u32[]{:S(2)}) collective-permute-start(bf16[128,2048]{1,0:T(8,128)(2,1)S(1)} %fusion.182), channel_id=1, source_target_pairs={{16,0},{17,1},{18,2},{19,3},{20,4},{21,5},{22,6},{23,7},{24,8},{25... | collective-permute-start | bytes 1572872 | tf_op jit(solution)/shard_map/ppermute | solution.py:10
  259.1 15.1 %collective-permute-start.15 = (bf16[128,2048]{1,0:T(8,128)(2,1)S(1)}, bf16[128,2048]{1,0:T(8,128)(2,1)S(1)}, u32[]{:S(2)}, u32[]{:S(2)}) collective-permute-start(bf16[128,2048]{1,0:T(8,128)(2,1)S(1)} %fusion.175), channel_id=1, source_target_pairs={{8,0},{9,1},{10,2},{11,3},{12,4},{13,5},{14,6},{15,7},{16,8},{17,9... | collective-permute-start | bytes 1572872 | tf_op jit(solution)/shard_map/ppermute | solution.py:10
  278.5 21.1 %collective-permute-start.16 = (bf16[128,2048]{1,0:T(8,128)(2,1)S(1)}, bf16[128,2048]{1,0:T(8,128)(2,1)S(1)}, u32[]{:S(2)}, u32[]{:S(2)}) collective-permute-start(bf16[128,2048]{1,0:T(8,128)(2,1)S(1)} %get-tuple-element.56), channel_id=1, source_target_pairs={{4,0},{5,1},{6,2},{7,3},{8,4},{9,5},{10,6},{11,7},{12,8},{13,9},{1... | collective-permute-start | bytes 1572872 | tf_op jit(solution)/shard_map/ppermute | solution.py:10
  303.0 33.5 %collective-permute-start.17 = (bf16[128,2048]{1,0:T(8,128)(2,1)S(1)}, bf16[128,2048]{1,0:T(8,128)(2,1)S(1)}, u32[]{:S(2)}, u32[]{:S(2)}) collective-permute-start(bf16[128,2048]{1,0:T(8,128)(2,1)S(1)} %get-tuple-element.57), channel_id=1, source_target_pairs={{2,0},{3,1},{4,2},{5,3},{6,4},{7,5},{8,6},{9,7},{10,8},{11,9},{12,... | collective-permute-start | bytes 1572872 | tf_op jit(solution)/shard_map/ppermute | solution.py:10
  340.0 8.6 %collective-permute-start.18 = (bf16[128,2048]{1,0:T(8,128)(2,1)S(1)}, bf16[128,2048]{1,0:T(8,128)(2,1)S(1)}, u32[]{:S(2)}, u32[]{:S(2)}) collective-permute-start(bf16[128,2048]{1,0:T(8,128)(2,1)S(1)} %get-tuple-element.58), channel_id=1, source_target_pairs={{1,0},{2,1},{3,2},{4,3},{5,4},{6,5},{7,6},{8,7},{9,8},{10,9},{11,1... | collective-permute-start | bytes 1572872 | tf_op jit(solution)/shard_map/ppermute | solution.py:10
  351.2 8.1 collective-permute-start.19
  361.8 9.7 %collective-permute-start.20 = (bf16[32,2048]{1,0:T(8,128)(2,1)S(1)}, bf16[32,2048]{1,0:T(8,128)(2,1)S(1)}, u32[]{:S(2)}, u32[]{:S(2)}) collective-permute-start(bf16[32,2048]{1,0:T(8,128)(2,1)S(1)} %slice.215), channel_id=1, source_target_pairs={{1,0},{2,1},{3,2},{4,3},{5,4},{6,5},{7,6},{8,7},{9,8},{10,9},{11,1... | collective-permute-start | bytes 393224 | tf_op jit(solution)/shard_map/ppermute | solution.py:10
  373.5 8.6 %collective-permute-start.21 = (bf16[16,2048]{1,0:T(8,128)(2,1)S(1)}, bf16[16,2048]{1,0:T(8,128)(2,1)S(1)}, u32[]{:S(2)}, u32[]{:S(2)}) collective-permute-start(bf16[16,2048]{1,0:T(8,128)(2,1)S(1)} %slice.217), channel_id=1, source_target_pairs={{1,0},{2,1},{3,2},{4,3},{5,4},{6,5},{7,6},{8,7},{9,8},{10,9},{11,1... | collective-permute-start | bytes 196616 | tf_op jit(solution)/shard_map/ppermute | solution.py:10
  384.0 5.5 collective-permute-start.22
  391.8 5.2 collective-permute-start.23
  399.1 112.1 %copy-start.91 = (f32[2048]{0:T(1024)S(1)}, f32[2048]{0:T(1024)}, u32[]{:S(2)}) copy-start(f32[2048]{0:T(1024)} %get-tuple-element.17) | copy-start | bytes 24580
  399.2 112.1 %copy-start.92 = (f32[2048]{0:T(1024)S(1)}, f32[2048]{0:T(1024)}, u32[]{:S(2)}) copy-start(f32[2048]{0:T(1024)} %get-tuple-element.52) | copy-start | bytes 24580
  399.2 113.6 %copy-start.28 = (f32[1,2048]{1,0:T(1,128)S(1)}, f32[1,2048]{1,0:T(1,128)}, u32[]{:S(2)}) copy-start(f32[1,2048]{1,0:T(1,128)} %get-tuple-element.84) | copy-start | bytes 24580
  399.2 5.2 collective-permute-start.24
  406.6 106.2 %collective-permute-start.25 = (bf16[1,2048]{1,0:T(2,128)(2,1)S(1)}, bf16[1,2048]{1,0:T(2,128)(2,1)S(1)}, u32[]{:S(2)}, u32[]{:S(2)}) collective-permute-start(bf16[1,2048]{1,0:T(2,128)(2,1)S(1)} %slice.225), channel_id=1, source_target_pairs={{1,0},{2,1},{3,2},{4,3},{5,4},{6,5},{7,6},{8,7},{9,8},{10,9},{11,1... | collective-permute-start | bytes 12296 | tf_op jit(solution)/shard_map/ppermute | solution.py:10
  512.7 289.9 %all-reduce.3.cloned.1.call-start = ((), (), s32[]{:S(2)}) async-start(), calls=%async_computation.2 | async-start | bytes 524288 | tf_op jit(solution)/shard_map/psum | solution.py:115
  (84 other events, 4780.8 us)
Sparse Core Ops, SparseCore 0:
  205.4 223.6 reduce-scatter.1
Sparse Core Ops, SparseCore 1:
  512.8 244.4 all-reduce.4
  759.4 43.2 all-reduce.2
where the time goes:
time: 819 us; the launch traced here: 812 us
  waiting for transfers between devices  489 us (60%)
  starting transfers between devices  124 us (15%)
  blocking collectives  102 us (12%)
  other arithmetic  58.4 us (7%)
  between operations  17.8 us (2%)
  matrix products  13.3 us (2%)
    psum x1, waiting for transfers between devices, body(): lax.psum((jnp.stack([theta, phi]), jnp.stack(mix_rows)), ('stream', 'seq'))  243 us
    ppermute x26, waiting for transfers between devices, from_behind(): return lax.ppermute(block, axis, route)  202 us
    ppermute x26, starting transfers between devices, from_behind(): return lax.ppermute(block, axis, route)  124 us
    psum x1, blocking collectives, body(): lax.psum((jnp.stack([theta, phi]), jnp.stack(mix_rows)), ('stream', 'seq'))  102 us
    psum x1, waiting for transfers between devices, body(): weight_rows = lax.psum(weight_rows, 'stream')  43.9 us
    reduce_sum x10, other arithmetic, body(): jnp.sum(grad_full * (cos_d * plain + sin_d * shifted), axis=0)  22.1 us
  transfers between devices with their start and end apart: 29, of which 26 were waited for; matrix products, arithmetic and copies ran while one was open for 6% of the time, Pallas kernels for 0%

commit v1 on v0

--- a/solution.py
+++ b/solution.py
@@ -1,7 +1,23 @@
+import functools
 import jax
 import jax.numpy as jnp
 from jax import lax
 from jax.sharding import PartitionSpec as P
+
+
+def recast_ends_over_axis(x_local, shard_axis):
+    n_parts = lax.axis_size(shard_axis)
+    mid_arr, found_now = (x_local, 0)
+    while 1 << found_now < n_parts:
+        arr_out = lax.ppermute(
+            mid_arr, shard_axis, [(s, s ^ 1 << found_now) for s in range(n_parts)]
+        )
+        mid_arr = mid_arr + arr_out
+        found_now = found_now + 1
+    return mid_arr
+
+
+pieces_all_recover = functools.partial(recast_ends_over_axis, shard_axis="stream")
 
 
 def from_behind(block, axis, distance):
@@ -112,7 +128,7 @@
         scatter_dimension=0,
         tiled=True,
     )
-    weight_rows = lax.psum(weight_rows, "stream")
+    weight_rows = pieces_all_recover(weight_rows)
     return (output[None], carried[None], weight_rows * factor, angle_all * factor, mix_all * factor)
 
 

time: 819 us -> 774 us (0.945)
  waiting for transfers between devices: 489 us -> 440 us
    psum x1 -> x0, waiting for transfers between devices: 43.9 us -> none  [body(): weight_rows = lax.psum(weight_rows, 'stream')]
    psum x1, waiting for transfers between devices: 243 us -> 233 us  [body(): lax.psum((jnp.stack([theta, phi]), jnp.stack(mix_rows)), ('stream', 'seq'))]
  transfers between devices with their start and end apart: 29 -> 30, of which waited for: 26 -> 26; matrix products, arithmetic and copies ran while one was open for 6% -> 6% of each run, Pallas kernels for 0% -> 0%
where the time goes in v1:
time: 774 us; the launch traced here: 767 us
  waiting for transfers between devices  440 us (57%)
  starting transfers between devices  128 us (17%)
  blocking collectives  102 us (13%)
  other arithmetic  58.4 us (8%)
  between operations  17.8 us (2%)
  matrix products  13.3 us (2%)
    psum x1, waiting for transfers between devices, body(): lax.psum((jnp.stack([theta, phi]), jnp.stack(mix_rows)), ('stream', 'seq'))  233 us
    ppermute x26, waiting for transfers between devices, from_behind(): return lax.ppermute(block, axis, route)  201 us
    ppermute x26, starting transfers between devices, from_behind(): return lax.ppermute(block, axis, route)  125 us
    psum x1, blocking collectives, body(): lax.psum((jnp.stack([theta, phi]), jnp.stack(mix_rows)), ('stream', 'seq'))  102 us
    reduce_sum x10, other arithmetic, body(): jnp.sum(grad_full * (cos_d * plain + sin_d * shifted), axis=0)  22.1 us
  transfers between devices with their start and end apart: 30, of which 26 were waited for; matrix products, arithmetic and copies ran while one was open for 6% of the time, Pallas kernels for 0%

profile of v1, /device:TPU:8, one launch (start us, length us, event | category | flops | bytes accessed | tf_op | source)
XLA Modules:
  0.0 767.1 jit_solution(10923832567938985907)
XLA Ops:
  17.4 3.6 collective-permute-start.1
  25.5 3.1 collective-permute-done.2
  31.6 3.3 collective-permute-done.3
  35.9 2.1 collective-permute-start.4
  38.0 3.6 collective-permute-done.4
  44.4 4.3 collective-permute-done.5
  51.6 5.8 collective-permute-done.6
  58.4 2.1 collective-permute-start.7
  60.5 8.6 %collective-permute-done.7 = bf16[128,2048]{1,0:T(8,128)(2,1)S(1)} collective-permute-done((bf16[128,2048]{1,0:T(8,128)(2,1)S(1)}, bf16[128,2048]{1,0:T(8,128)(2,1)S(1)}, u32[]{:S(2)}, u32[]{:S(2)}) %collective-permute-start.7) | collective-permute-done | bytes 524320 | tf_op jit(solution)/shard_map/ppermute | solution.py:26
  70.1 3.5 collective-permute-start.8
  73.6 11.4 %collective-permute-done.8 = bf16[128,2048]{1,0:T(8,128)(2,1)S(1)} collective-permute-done((bf16[128,2048]{1,0:T(8,128)(2,1)S(1)}, bf16[128,2048]{1,0:T(8,128)(2,1)S(1)}, u32[]{:S(2)}, u32[]{:S(2)}) %collective-permute-start.8) | collective-permute-done | bytes 524320 | tf_op jit(solution)/shard_map/ppermute | solution.py:26
  86.0 15.0 %collective-permute-start.9 = (bf16[128,2048]{1,0:T(8,128)(2,1)S(1)}, bf16[128,2048]{1,0:T(8,128)(2,1)S(1)}, u32[]{:S(2)}, u32[]{:S(2)}) collective-permute-start(bf16[128,2048]{1,0:T(8,128)(2,1)S(1)} %fusion.250), channel_id=1, source_target_pairs={{0,4},{1,5},{2,6},{3,7},{4,8},{5,9},{6,10},{7,11},{8,12},{9,13},{1... | collective-permute-start | bytes 1572872 | tf_op jit(solution)/shard_map/ppermute | solution.py:26
  101.0 7.5 collective-permute-done.9
  109.4 4.4 collective-permute-start.10
  113.7 6.6 collective-permute-done.10
  121.3 14.6 %collective-permute-start.11 = (bf16[128,2048]{1,0:T(8,128)(2,1)S(1)}, bf16[128,2048]{1,0:T(8,128)(2,1)S(1)}, u32[]{:S(2)}, u32[]{:S(2)}) collective-permute-start(bf16[128,2048]{1,0:T(8,128)(2,1)S(1)} %fusion.254), channel_id=1, source_target_pairs={{0,16},{1,17},{2,18},{3,19},{4,20},{5,21},{6,22},{7,23},{8,24},{9,... | collective-permute-start | bytes 1572872 | tf_op jit(solution)/shard_map/ppermute | solution.py:26
  135.9 8.1 %collective-permute-done.11 = bf16[128,2048]{1,0:T(8,128)(2,1)S(1)} collective-permute-done((bf16[128,2048]{1,0:T(8,128)(2,1)S(1)}, bf16[128,2048]{1,0:T(8,128)(2,1)S(1)}, u32[]{:S(2)}, u32[]{:S(2)}) %collective-permute-start.11) | collective-permute-done | bytes 524320 | tf_op jit(solution)/shard_map/ppermute | solution.py:26
  144.9 31.3 %collective-permute-start.12 = (bf16[128,2048]{1,0:T(8,128)(2,1)S(1)}, bf16[128,2048]{1,0:T(8,128)(2,1)S(1)}, u32[]{:S(2)}, u32[]{:S(2)}) collective-permute-start(bf16[128,2048]{1,0:T(8,128)(2,1)S(1)} %fusion.256), channel_id=1, source_target_pairs={{0,32},{1,33},{2,34},{3,35},{4,36},{5,37},{6,38},{7,39},{8,40},{9,... | collective-permute-start | bytes 1572872 | tf_op jit(solution)/shard_map/ppermute | solution.py:26
  176.3 2.9 convolution_convert_fusion
  179.4 7.8 %collective-permute-done.12 = bf16[128,2048]{1,0:T(8,128)(2,1)S(1)} collective-permute-done((bf16[128,2048]{1,0:T(8,128)(2,1)S(1)}, bf16[128,2048]{1,0:T(8,128)(2,1)S(1)}, u32[]{:S(2)}, u32[]{:S(2)}) %collective-permute-start.12) | collective-permute-done | bytes 524320 | tf_op jit(solution)/shard_map/ppermute | solution.py:26
  188.4 7.4 fusion.97
  197.0 8.1 %fusion.288 = f32[2048,2048]{1,0:T(8,128)} fusion(bf16[1,128,2048]{2,1,0:T(8,128)(2,1)S(1)} %copy-done, f32[128,2048]{1,0:T(8,128)S(1)} %get-tuple-element.55), kind=kOutput, calls=%fused_computation.471 | convolution fusion | flops 1076101120 | bytes 18350080 | tf_op jit(solution)/shard_map/dot_general | solution.py:124
  207.9 19.4 %collective-permute-done.13 = bf16[128,2048]{1,0:T(8,128)(2,1)S(1)} collective-permute-done((bf16[128,2048]{1,0:T(8,128)(2,1)S(1)}, bf16[128,2048]{1,0:T(8,128)(2,1)S(1)}, u32[]{:S(2)}, u32[]{:S(2)}) %collective-permute-start.13) | collective-permute-done | bytes 524320 | tf_op jit(solution)/shard_map/ppermute | solution.py:26
  230.6 26.2 %collective-permute-done.14 = bf16[128,2048]{1,0:T(8,128)(2,1)S(1)} collective-permute-done((bf16[128,2048]{1,0:T(8,128)(2,1)S(1)}, bf16[128,2048]{1,0:T(8,128)(2,1)S(1)}, u32[]{:S(2)}, u32[]{:S(2)}) %collective-permute-start.14) | collective-permute-done | bytes 524320 | tf_op jit(solution)/shard_map/ppermute | solution.py:26
  260.5 13.7 %collective-permute-done.15 = bf16[128,2048]{1,0:T(8,128)(2,1)S(1)} collective-permute-done((bf16[128,2048]{1,0:T(8,128)(2,1)S(1)}, bf16[128,2048]{1,0:T(8,128)(2,1)S(1)}, u32[]{:S(2)}, u32[]{:S(2)}) %collective-permute-start.15) | collective-permute-done | bytes 524320 | tf_op jit(solution)/shard_map/ppermute | solution.py:26
  275.3 3.1 fusion.270
  279.7 19.8 %collective-permute-done.16 = bf16[128,2048]{1,0:T(8,128)(2,1)S(1)} collective-permute-done((bf16[128,2048]{1,0:T(8,128)(2,1)S(1)}, bf16[128,2048]{1,0:T(8,128)(2,1)S(1)}, u32[]{:S(2)}, u32[]{:S(2)}) %collective-permute-start.16) | collective-permute-done | bytes 524320 | tf_op jit(solution)/shard_map/ppermute | solution.py:26
  299.9 3.1 fusion.269
  302.9 10.8 %collective-permute-start.17 = (bf16[128,2048]{1,0:T(8,128)(2,1)S(1)}, bf16[128,2048]{1,0:T(8,128)(2,1)S(1)}, u32[]{:S(2)}, u32[]{:S(2)}) collective-permute-start(bf16[128,2048]{1,0:T(8,128)(2,1)S(1)} %get-tuple-element.57), channel_id=1, source_target_pairs={{2,0},{3,1},{4,2},{5,3},{6,4},{7,5},{8,6},{9,7},{10,8},{11,9},{12,... | collective-permute-start | bytes 1572872 | tf_op jit(solution)/shard_map/ppermute | solution.py:26
  313.7 22.7 %collective-permute-done.17 = bf16[128,2048]{1,0:T(8,128)(2,1)S(1)} collective-permute-done((bf16[128,2048]{1,0:T(8,128)(2,1)S(1)}, bf16[128,2048]{1,0:T(8,128)(2,1)S(1)}, u32[]{:S(2)}, u32[]{:S(2)}) %collective-permute-start.17) | collective-permute-done | bytes 524320 | tf_op jit(solution)/shard_map/ppermute | solution.py:26
  336.9 3.0 fusion.268
  341.8 6.7 collective-permute-done.18
  348.9 2.2 fusion.267
  351.1 4.2 collective-permute-start.19
  355.4 3.9 collective-permute-done.19
  359.6 2.2 fusion.266
  361.8 4.2 collective-permute-start.20
  366.1 4.8 collective-permute-done.20
  372.8 3.9 collective-permute-start.21
  376.8 4.5 collective-permute-done.21
  385.2 3.6 collective-permute-done.22
  393.0 3.1 collective-permute-done.23
  398.4 2.1 collective-permute-start.24
  400.5 2.3 fusion
  408.1 102.1 %psum.14 = f32[2,2048]{1,0:T(2,128)S(1)} all-reduce(f32[2,2048]{1,0:T(2,128)S(1)} %pad_maximum_fusion.7), channel_id=1, replica_groups=mesh['stream'=4,'seq'=64] {'stream','seq'}, use_global_device_ids=true, to_apply=%region_29.30 | all-reduce | flops 4096 | bytes 32768 | tf_op jit(solution)/shard_map/psum | solution.py:122
  514.7 6.2 collective-permute-done.26
  521.9 2.2 collective-permute-start.27
  524.2 233.0 %all-reduce.2.cloned.1.call-done = f32[14,2048]{1,0:T(8,128)} async-done(((f32[14,2048]{1,0:T(8,128)}), f32[14,2048]{1,0:T(8,128)}) %all-reduce.2.cloned.1.call-update) | async-done | bytes 114704 | tf_op jit(solution)/shard_map/psum | solution.py:122
  (304 shorter events, 71.2 us)
Async XLA Ops:
  8.0 168.2 %copy-start = (bf16[1,128,2048]{2,1,0:T(8,128)(2,1)S(1)}, bf16[1,128,2048]{2,1,0:T(8,128)(2,1)}, u32[]{:S(2)}) copy-start(bf16[1,128,2048]{2,1,0:T(8,128)(2,1)} %param.7) | copy-start | bytes 1572868
  8.0 504.5 %reduce-scatter.2.cloned.1.call-start = ((), (), s32[]{:S(2)}) async-start(), calls=%async_computation.1 | async-start | bytes 17039360 | tf_op jit(solution)/shard_map/reduce_scatter | solution.py:123
  8.9 7.1 collective-permute-start
  17.4 5.1 collective-permute-start.1
  23.6 5.1 collective-permute-start.2
  28.6 159.5 %copy-start.65 = (bf16[4,2048]{1,0:T(4,128)(2,1)}, bf16[4,2048]{1,0:T(4,128)(2,1)S(1)}, u32[]{:S(2)}) copy-start(bf16[4,2048]{1,0:T(4,128)(2,1)S(1)} %collective-permute-done.2) | copy-start | bytes 49156
  29.6 5.2 collective-permute-start.3
  31.6 156.6 %copy-start.22 = (bf16[120,2048]{1,0:T(8,128)(2,1)}, bf16[120,2048]{1,0:T(8,128)(2,1)S(1)}, u32[]{:S(2)}) copy-start(bf16[120,2048]{1,0:T(8,128)(2,1)S(1)} %slice.205) | copy-start | bytes 1474564
  34.8 153.4 %copy-start.55 = (bf16[8,2048]{1,0:T(8,128)(2,1)}, bf16[8,2048]{1,0:T(8,128)(2,1)S(1)}, u32[]{:S(2)}) copy-start(bf16[8,2048]{1,0:T(8,128)(2,1)S(1)} %collective-permute-done.3) | copy-start | bytes 98308
  34.8 141.4 %slice-start = ((s8[8388608]{0:T(1024)(128)(4,1)}), s8[4194304]{0:T(1024)(128)(4,1)S(1)}, s32[]{:S(2)}) async-start(s8[8388608]{0:T(1024)(128)(4,1)} %bitcast.103), calls=%async_computation.3 | async-start | bytes 8388608
  35.9 5.7 collective-permute-start.4
  38.0 150.2 %copy-start.24 = (bf16[112,2048]{1,0:T(8,128)(2,1)}, bf16[112,2048]{1,0:T(8,128)(2,1)S(1)}, u32[]{:S(2)}) copy-start(bf16[112,2048]{1,0:T(8,128)(2,1)S(1)} %slice.207) | copy-start | bytes 1376260
  41.6 146.6 %copy-start.53 = (bf16[16,2048]{1,0:T(8,128)(2,1)}, bf16[16,2048]{1,0:T(8,128)(2,1)S(1)}, u32[]{:S(2)}) copy-start(bf16[16,2048]{1,0:T(8,128)(2,1)S(1)} %collective-permute-done.4) | copy-start | bytes 196612
  42.4 145.8 %copy-start.1 = (bf16[128,2048]{1,0:T(8,128)(2,1)}, bf16[128,2048]{1,0:T(8,128)(2,1)S(1)}, u32[]{:S(2)}) copy-start(bf16[128,2048]{1,0:T(8,128)(2,1)S(1)} %fusion.242) | copy-start | bytes 1572868
  42.5 6.3 collective-permute-start.5
  48.8 139.5 %copy-start.51 = (bf16[32,2048]{1,0:T(8,128)(2,1)}, bf16[32,2048]{1,0:T(8,128)(2,1)S(1)}, u32[]{:S(2)}) copy-start(bf16[32,2048]{1,0:T(8,128)(2,1)S(1)} %collective-permute-done.5) | copy-start | bytes 393220
  49.6 138.6 %copy-start.3 = (bf16[128,2048]{1,0:T(8,128)(2,1)}, bf16[128,2048]{1,0:T(8,128)(2,1)S(1)}, u32[]{:S(2)}) copy-start(bf16[128,2048]{1,0:T(8,128)(2,1)S(1)} %fusion.244) | copy-start | bytes 1572868
  49.7 138.6 %copy-start.43 = (bf16[64,2048]{1,0:T(8,128)(2,1)}, bf16[64,2048]{1,0:T(8,128)(2,1)S(1)}, u32[]{:S(2)}) copy-start(bf16[64,2048]{1,0:T(8,128)(2,1)S(1)} %get-tuple-element.69) | copy-start | bytes 786436
  49.7 7.7 %collective-permute-start.6 = (bf16[64,2048]{1,0:T(8,128)(2,1)S(1)}, bf16[64,2048]{1,0:T(8,128)(2,1)S(1)}, u32[]{:S(2)}, u32[]{:S(2)}) collective-permute-start(bf16[64,2048]{1,0:T(8,128)(2,1)S(1)} %get-tuple-element.68), channel_id=1, source_target_pairs={{0,1},{1,2},{2,3},{3,4},{4,5},{5,6},{6,7},{7,8},{8,9},{9,10},{10,1... | collective-permute-start | bytes 786440 | tf_op jit(solution)/shard_map/ppermute | solution.py:26
  57.4 130.9 %copy-start.47 = (bf16[64,2048]{1,0:T(8,128)(2,1)}, bf16[64,2048]{1,0:T(8,128)(2,1)S(1)}, u32[]{:S(2)}) copy-start(bf16[64,2048]{1,0:T(8,128)(2,1)S(1)} %collective-permute-done.6) | copy-start | bytes 786436
  57.4 118.8 %slice-start.1 = ((s8[8388608]{0:T(1024)(128)(4,1)}), s8[4194304]{0:T(1024)(128)(4,1)S(1)}, s32[]{:S(2)}) async-start(s8[8388608]{0:T(1024)(128)(4,1)} %bitcast.103), calls=%async_computation.4 | async-start | bytes 8388608
  58.4 129.9 %copy-start.18 = (bf16[128,2048]{1,0:T(8,128)(2,1)}, bf16[128,2048]{1,0:T(8,128)(2,1)S(1)}, u32[]{:S(2)}) copy-start(bf16[128,2048]{1,0:T(8,128)(2,1)S(1)} %fusion.246) | copy-start | bytes 1572868
  58.4 10.6 %collective-permute-start.7 = (bf16[128,2048]{1,0:T(8,128)(2,1)S(1)}, bf16[128,2048]{1,0:T(8,128)(2,1)S(1)}, u32[]{:S(2)}, u32[]{:S(2)}) collective-permute-start(bf16[128,2048]{1,0:T(8,128)(2,1)S(1)} %fusion.246), channel_id=1, source_target_pairs={{0,1},{1,2},{2,3},{3,4},{4,5},{5,6},{6,7},{7,8},{8,9},{9,10},{10,1... | collective-permute-start | bytes 1572872 | tf_op jit(solution)/shard_map/ppermute | solution.py:26
  69.1 119.2 %copy-start.39 = (bf16[128,2048]{1,0:T(8,128)(2,1)}, bf16[128,2048]{1,0:T(8,128)(2,1)S(1)}, u32[]{:S(2)}) copy-start(bf16[128,2048]{1,0:T(8,128)(2,1)S(1)} %collective-permute-done.7) | copy-start | bytes 1572868
  70.0 118.2 %copy-start.7 = (bf16[128,2048]{1,0:T(8,128)(2,1)}, bf16[128,2048]{1,0:T(8,128)(2,1)S(1)}, u32[]{:S(2)}) copy-start(bf16[128,2048]{1,0:T(8,128)(2,1)S(1)} %fusion.248) | copy-start | bytes 1572868
  70.1 14.9 %collective-permute-start.8 = (bf16[128,2048]{1,0:T(8,128)(2,1)S(1)}, bf16[128,2048]{1,0:T(8,128)(2,1)S(1)}, u32[]{:S(2)}, u32[]{:S(2)}) collective-permute-start(bf16[128,2048]{1,0:T(8,128)(2,1)S(1)} %fusion.248), channel_id=1, source_target_pairs={{0,2},{1,3},{2,4},{3,5},{4,6},{5,7},{6,8},{7,9},{8,10},{9,11},{10,... | collective-permute-start | bytes 1572872 | tf_op jit(solution)/shard_map/ppermute | solution.py:26
  86.0 22.5 %collective-permute-start.9 = (bf16[128,2048]{1,0:T(8,128)(2,1)S(1)}, bf16[128,2048]{1,0:T(8,128)(2,1)S(1)}, u32[]{:S(2)}, u32[]{:S(2)}) collective-permute-start(bf16[128,2048]{1,0:T(8,128)(2,1)S(1)} %fusion.250), channel_id=1, source_target_pairs={{0,4},{1,5},{2,6},{3,7},{4,8},{5,9},{6,10},{7,11},{8,12},{9,13},{1... | collective-permute-start | bytes 1572872 | tf_op jit(solution)/shard_map/ppermute | solution.py:26
  109.4 11.0 %collective-permute-start.10 = (bf16[128,2048]{1,0:T(8,128)(2,1)S(1)}, bf16[128,2048]{1,0:T(8,128)(2,1)S(1)}, u32[]{:S(2)}, u32[]{:S(2)}) collective-permute-start(bf16[128,2048]{1,0:T(8,128)(2,1)S(1)} %fusion.252), channel_id=1, source_target_pairs={{0,8},{1,9},{2,10},{3,11},{4,12},{5,13},{6,14},{7,15},{8,16},{9,17... | collective-permute-start | bytes 1572872 | tf_op jit(solution)/shard_map/ppermute | solution.py:26
  121.3 22.6 %collective-permute-start.11 = (bf16[128,2048]{1,0:T(8,128)(2,1)S(1)}, bf16[128,2048]{1,0:T(8,128)(2,1)S(1)}, u32[]{:S(2)}, u32[]{:S(2)}) collective-permute-start(bf16[128,2048]{1,0:T(8,128)(2,1)S(1)} %fusion.254), channel_id=1, source_target_pairs={{0,16},{1,17},{2,18},{3,19},{4,20},{5,21},{6,22},{7,23},{8,24},{9,... | collective-permute-start | bytes 1572872 | tf_op jit(solution)/shard_map/ppermute | solution.py:26
  144.9 42.4 %collective-permute-start.12 = (bf16[128,2048]{1,0:T(8,128)(2,1)S(1)}, bf16[128,2048]{1,0:T(8,128)(2,1)S(1)}, u32[]{:S(2)}, u32[]{:S(2)}) collective-permute-start(bf16[128,2048]{1,0:T(8,128)(2,1)S(1)} %fusion.256), channel_id=1, source_target_pairs={{0,32},{1,33},{2,34},{3,35},{4,36},{5,37},{6,38},{7,39},{8,40},{9,... | collective-permute-start | bytes 1572872 | tf_op jit(solution)/shard_map/ppermute | solution.py:26
  205.2 552.0 %all-reduce.2.cloned.1.call-start = ((), (), s32[]{:S(2)}) async-start(), calls=%async_computation.2 | async-start | bytes 262144 | tf_op jit(solution)/shard_map/psum | solution.py:122
  206.5 20.8 %collective-permute-start.13 = (bf16[128,2048]{1,0:T(8,128)(2,1)S(1)}, bf16[128,2048]{1,0:T(8,128)(2,1)S(1)}, u32[]{:S(2)}, u32[]{:S(2)}) collective-permute-start(bf16[128,2048]{1,0:T(8,128)(2,1)S(1)} %fusion.189), channel_id=1, source_target_pairs={{32,0},{33,1},{34,2},{35,3},{36,4},{37,5},{38,6},{39,7},{40,8},{41... | collective-permute-start | bytes 1572872 | tf_op jit(solution)/shard_map/ppermute | solution.py:26
  229.3 27.5 %collective-permute-start.14 = (bf16[128,2048]{1,0:T(8,128)(2,1)S(1)}, bf16[128,2048]{1,0:T(8,128)(2,1)S(1)}, u32[]{:S(2)}, u32[]{:S(2)}) collective-permute-start(bf16[128,2048]{1,0:T(8,128)(2,1)S(1)} %fusion.182), channel_id=1, source_target_pairs={{16,0},{17,1},{18,2},{19,3},{20,4},{21,5},{22,6},{23,7},{24,8},{25... | collective-permute-start | bytes 1572872 | tf_op jit(solution)/shard_map/ppermute | solution.py:26
  259.0 15.1 %collective-permute-start.15 = (bf16[128,2048]{1,0:T(8,128)(2,1)S(1)}, bf16[128,2048]{1,0:T(8,128)(2,1)S(1)}, u32[]{:S(2)}, u32[]{:S(2)}) collective-permute-start(bf16[128,2048]{1,0:T(8,128)(2,1)S(1)} %fusion.175), channel_id=1, source_target_pairs={{8,0},{9,1},{10,2},{11,3},{12,4},{13,5},{14,6},{15,7},{16,8},{17,9... | collective-permute-start | bytes 1572872 | tf_op jit(solution)/shard_map/ppermute | solution.py:26
  278.4 21.1 %collective-permute-start.16 = (bf16[128,2048]{1,0:T(8,128)(2,1)S(1)}, bf16[128,2048]{1,0:T(8,128)(2,1)S(1)}, u32[]{:S(2)}, u32[]{:S(2)}) collective-permute-start(bf16[128,2048]{1,0:T(8,128)(2,1)S(1)} %get-tuple-element.56), channel_id=1, source_target_pairs={{4,0},{5,1},{6,2},{7,3},{8,4},{9,5},{10,6},{11,7},{12,8},{13,9},{1... | collective-permute-start | bytes 1572872 | tf_op jit(solution)/shard_map/ppermute | solution.py:26
  302.9 33.5 %collective-permute-start.17 = (bf16[128,2048]{1,0:T(8,128)(2,1)S(1)}, bf16[128,2048]{1,0:T(8,128)(2,1)S(1)}, u32[]{:S(2)}, u32[]{:S(2)}) collective-permute-start(bf16[128,2048]{1,0:T(8,128)(2,1)S(1)} %get-tuple-element.57), channel_id=1, source_target_pairs={{2,0},{3,1},{4,2},{5,3},{6,4},{7,5},{8,6},{9,7},{10,8},{11,9},{12,... | collective-permute-start | bytes 1572872 | tf_op jit(solution)/shard_map/ppermute | solution.py:26
  339.9 8.6 %collective-permute-start.18 = (bf16[128,2048]{1,0:T(8,128)(2,1)S(1)}, bf16[128,2048]{1,0:T(8,128)(2,1)S(1)}, u32[]{:S(2)}, u32[]{:S(2)}) collective-permute-start(bf16[128,2048]{1,0:T(8,128)(2,1)S(1)} %get-tuple-element.58), channel_id=1, source_target_pairs={{1,0},{2,1},{3,2},{4,3},{5,4},{6,5},{7,6},{8,7},{9,8},{10,9},{11,1... | collective-permute-start | bytes 1572872 | tf_op jit(solution)/shard_map/ppermute | solution.py:26
  351.1 8.1 %collective-permute-start.19 = (bf16[64,2048]{1,0:T(8,128)(2,1)S(1)}, bf16[64,2048]{1,0:T(8,128)(2,1)S(1)}, u32[]{:S(2)}, u32[]{:S(2)}) collective-permute-start(bf16[64,2048]{1,0:T(8,128)(2,1)S(1)} %get-tuple-element.67), channel_id=1, source_target_pairs={{1,0},{2,1},{3,2},{4,3},{5,4},{6,5},{7,6},{8,7},{9,8},{10,9},{11,1... | collective-permute-start | bytes 786440 | tf_op jit(solution)/shard_map/ppermute | solution.py:26
  361.8 9.1 %collective-permute-start.20 = (bf16[32,2048]{1,0:T(8,128)(2,1)S(1)}, bf16[32,2048]{1,0:T(8,128)(2,1)S(1)}, u32[]{:S(2)}, u32[]{:S(2)}) collective-permute-start(bf16[32,2048]{1,0:T(8,128)(2,1)S(1)} %slice.215), channel_id=1, source_target_pairs={{1,0},{2,1},{3,2},{4,3},{5,4},{6,5},{7,6},{8,7},{9,8},{10,9},{11,1... | collective-permute-start | bytes 393224 | tf_op jit(solution)/shard_map/ppermute | solution.py:26
  372.8 8.5 %collective-permute-start.21 = (bf16[16,2048]{1,0:T(8,128)(2,1)S(1)}, bf16[16,2048]{1,0:T(8,128)(2,1)S(1)}, u32[]{:S(2)}, u32[]{:S(2)}) collective-permute-start(bf16[16,2048]{1,0:T(8,128)(2,1)S(1)} %slice.217), channel_id=1, source_target_pairs={{1,0},{2,1},{3,2},{4,3},{5,4},{6,5},{7,6},{8,7},{9,8},{10,9},{11,1... | collective-permute-start | bytes 196616 | tf_op jit(solution)/shard_map/ppermute | solution.py:26
  383.3 5.5 collective-permute-start.22
  390.9 5.2 collective-permute-start.23
  398.3 112.7 %copy-start.91 = (f32[2048]{0:T(1024)S(1)}, f32[2048]{0:T(1024)}, u32[]{:S(2)}) copy-start(f32[2048]{0:T(1024)} %get-tuple-element.17) | copy-start | bytes 24580
  398.4 115.2 %copy-start.28 = (f32[1,2048]{1,0:T(1,128)S(1)}, f32[1,2048]{1,0:T(1,128)}, u32[]{:S(2)}) copy-start(f32[1,2048]{1,0:T(1,128)} %get-tuple-element.84) | copy-start | bytes 24580
  398.4 5.4 collective-permute-start.24
  406.0 107.5 %collective-permute-start.25 = (bf16[1,2048]{1,0:T(2,128)(2,1)S(1)}, bf16[1,2048]{1,0:T(2,128)(2,1)S(1)}, u32[]{:S(2)}, u32[]{:S(2)}) collective-permute-start(bf16[1,2048]{1,0:T(2,128)(2,1)S(1)} %slice.225), channel_id=1, source_target_pairs={{1,0},{2,1},{3,2},{4,3},{5,4},{6,5},{7,6},{8,7},{9,8},{10,9},{11,1... | collective-permute-start | bytes 12296 | tf_op jit(solution)/shard_map/ppermute | solution.py:26
  512.6 8.4 %collective-permute-start.26 = (f32[32,2048]{1,0:T(8,128)}, f32[32,2048]{1,0:T(8,128)S(1)}, u32[]{:S(2)}, u32[]{:S(2)}) collective-permute-start(f32[32,2048]{1,0:T(8,128)} %reduce-scatter.2.cloned.1.call-done), channel_id=1, source_target_pairs={{0,64},{64,0},{128,192},{192,128},{1,65},{65,1},{129,193},{193,129... | collective-permute-start | bytes 786440 | tf_op jit(solution)/shard_map/ppermute | solution.py:12
  521.9 236.8 %collective-permute-start.27 = (f32[32,2048]{1,0:T(8,128)S(1)}, f32[32,2048]{1,0:T(8,128)S(1)}, u32[]{:S(2)}, u32[]{:S(2)}) collective-permute-start(f32[32,2048]{1,0:T(8,128)S(1)} %add.742), channel_id=1, source_target_pairs={{0,128},{64,192},{128,0},{192,64},{1,129},{65,193},{129,1},{193,65... | collective-permute-start | bytes 786440 | tf_op jit(solution)/shard_map/ppermute | solution.py:12
  (85 other events, 4891.9 us)
Sparse Core Ops, SparseCore 0:
  205.3 223.6 reduce-scatter.1
Sparse Core Ops, SparseCore 1:
  512.6 244.4 all-reduce.1
